TPU v7x, 32 devices: a whole 2x2x4 slice. The times are simulated.
32 devices in a mesh: expert: 8 (over y, x, core), dp: 4 (over z).
Axes of the slice: x: 2, y: 2, z: 4, core: 2. Of those that a mesh axis runs over, the one named last changes fastest.
Arguments:
- tokens: bfloat16 [4096, 2048], P(('expert', 'dp')), may hold values from -6 to 6
- expert_ids: int32 [4096, 8], P(('expert', 'dp')), may hold values from 0 to 15, all different within a row; in each aligned block of 128 rows (0 to 127, 128 to 255, ...) at most 72 rows name the same one
- router: bfloat16 [2048, 16], replicated, may hold values from -0.25 to 0.25
- w_gate: bfloat16 [16, 2048, 640], P('expert'), may hold values from -0.125 to 0.125
- w_up: bfloat16 [16, 2048, 640], P('expert'), may hold values from -0.125 to 0.125
- w_down: bfloat16 [16, 640, 2048], P('expert'), may hold values from -1 to 1
- out_grad: bfloat16 [4096, 2048], P(('expert', 'dp')), may hold values from -6 to 6
Outputs:
- mixed: bfloat16 [4096, 2048], P(('expert', 'dp'))
- token_grad: bfloat16 [4096, 2048], P(('expert', 'dp'))
- router_grad: float32 [2048, 16], replicated
- gate_grad: bfloat16 [16, 2048, 640], P('expert', 'dp')
- up_grad: bfloat16 [16, 2048, 640], P('expert', 'dp')
- down_grad: bfloat16 [16, 640, 2048], P('expert', None, 'dp')
Inputs may be any that keep to these rules, and one draw needn't show every extreme that they name: `expert_ids`: each row names 8 different experts; within the 128 rows of one device no expert is named more than 72 times.
All inputs are finite; a program needn't handle non-finite values.
Results may differ from a plain program's by a relative error of at most 0.008.
Values may be sent and summed in bfloat16 or wider, within the bound.
No kernel may reach another device: no remote copies, remote signals or barrier semaphores. Data moves between devices by JAX's collectives and lax.ppermute only.
A program may use at most 256 MiB of HBM per device.

v0:
```python
import jax
import jax.numpy as jnp
from jax import lax
from jax.sharding import PartitionSpec as P


def flat_rows(array):
    return array.reshape(array.shape[0], array.shape[1] * array.shape[2], array.shape[3])


def body(tokens, expert_ids, router, w_gate, w_up, w_down, out_grad):
    f32 = jnp.float32
    bf16 = jnp.bfloat16
    tok_dev, width = tokens.shape
    top = expert_ids.shape[1]
    n_experts = router.shape[1]
    local_experts = w_gate.shape[0]
    groups = lax.axis_size("expert")
    capacity = (tok_dev * top * 9 + 8 * n_experts - 1) // (8 * n_experts)
    n_assign = tok_dev * top
    flat_ids = expert_ids.reshape(-1)
    ladder = jnp.arange(n_experts, dtype=jnp.int32)
    onehot = (flat_ids[:, None] == ladder[None, :]).astype(jnp.int32)
    rank = jnp.sum((jnp.cumsum(onehot, axis=0) - onehot) * onehot, axis=1)
    owner = flat_ids // local_experts
    within = flat_ids % local_experts
    dest = (within * groups + owner) * capacity + rank
    slot_src = jnp.full((n_experts * capacity,), n_assign, jnp.int32)
    slot_src = slot_src.at[dest].set(jnp.arange(n_assign, dtype=jnp.int32))
    live = slot_src < n_assign
    slot_tok = jnp.where(live, slot_src // top, 0)
    logits = jnp.dot(tokens, router, preferred_element_type=f32)
    scores = jax.nn.sigmoid(logits)
    chosen = jnp.take_along_axis(scores, expert_ids, axis=1)
    total = jnp.sum(chosen, axis=1, keepdims=True)
    gates = chosen / total
    gate_slots = jnp.where(live, gates.reshape(-1)[jnp.minimum(slot_src, n_assign - 1)], 0.0)
    send = jnp.where(live[:, None], tokens[slot_tok], jnp.zeros((), bf16))
    send = send.reshape(local_experts, groups, capacity, width)
    piece = lax.all_to_all(send, "expert", split_axis=1, concat_axis=1, tiled=True)
    shape = piece.shape
    rows = flat_rows(piece)
    pre_gate = jnp.einsum("jrd,jdf->jrf", rows, w_gate, preferred_element_type=f32)
    pre_up = jnp.einsum("jrd,jdf->jrf", rows, w_up, preferred_element_type=f32)
    hidden = (pre_gate * jax.nn.sigmoid(pre_gate) * pre_up).astype(bf16)
    expert_out = jnp.einsum("jrf,jfd->jrd", hidden, w_down, preferred_element_type=f32).astype(bf16)
    hid_shape = (shape[0], shape[1], shape[2], hidden.shape[2])
    expert_out = expert_out.reshape(shape)
    hidden = hidden.reshape(hid_shape)
    results = (expert_out, hidden, piece, pre_gate.reshape(hid_shape), pre_up.reshape(hid_shape))
    expert_out = results[0]
    hidden = flat_rows(results[1])
    back = lax.all_to_all(expert_out, "expert", split_axis=1, concat_axis=1, tiled=True).reshape(
        n_experts * capacity, width
    )
    picked = back[dest].reshape(tok_dev, top, width)
    mixed = jnp.einsum("tk,tkd->td", gates, picked.astype(f32)).astype(bf16)
    gate_sens = jnp.einsum("tkd,td->tk", picked, out_grad, preferred_element_type=f32)
    grad_rows = (gate_slots[:, None] * out_grad[slot_tok].astype(f32)).astype(bf16)
    grad_send = jnp.where(live[:, None], grad_rows, jnp.zeros((), bf16))
    grad_send = grad_send.reshape(local_experts, groups, capacity, width)
    grad_in4 = lax.all_to_all(grad_send, "expert", split_axis=1, concat_axis=1, tiled=True)
    grad_in = flat_rows(grad_in4)
    pre_gate = flat_rows(results[3])
    pre_up = flat_rows(results[4])
    hidden_grad = jnp.einsum("jrd,jfd->jrf", grad_in, w_down, preferred_element_type=f32)
    sig = jax.nn.sigmoid(pre_gate)
    silu_val = pre_gate * sig
    gate_term = (hidden_grad * pre_up * sig * (1.0 + pre_gate * (1.0 - sig))).astype(bf16)
    up_term = (hidden_grad * silu_val).astype(bf16)
    input_grad = (
        jnp.einsum("jrf,jdf->jrd", gate_term, w_gate, preferred_element_type=f32)
        + jnp.einsum("jrf,jdf->jrd", up_term, w_up, preferred_element_type=f32)
    ).astype(bf16)
    input_grad = input_grad.reshape(grad_in4.shape)
    returned = lax.all_to_all(
        input_grad, "expert", split_axis=1, concat_axis=1, tiled=True
    ).reshape(n_experts * capacity, width)
    moe_grad = jnp.sum(returned[dest].reshape(tok_dev, top, width).astype(f32), axis=1)
    chosen_grad = (gate_sens - jnp.sum(gate_sens * gates, axis=1, keepdims=True)) / total
    sel_grad = chosen_grad * chosen * (1.0 - chosen)
    pick = (expert_ids[:, :, None] == ladder[None, None, :]).astype(f32)
    logit_grad = jnp.einsum("tk,tke->te", sel_grad, pick).astype(bf16)
    token_grad = (moe_grad + jnp.dot(logit_grad, router.T, preferred_element_type=f32)).astype(bf16)
    router_grad = lax.psum(
        jnp.dot(tokens.T, logit_grad, preferred_element_type=f32), ("expert", "dp")
    )
    hidden_width = hidden.shape[2]
    arrived4 = results[2]
    columns = (
        lax.all_to_all(arrived4, "dp", split_axis=3, concat_axis=1, tiled=True),
        lax.all_to_all(grad_in4, "dp", split_axis=3, concat_axis=1, tiled=True),
    )
    hid_shape = (local_experts, groups, capacity, hidden_width)
    hiddens = (
        lax.all_gather(gate_term.reshape(hid_shape), "dp", axis=1, tiled=True),
        lax.all_gather(up_term.reshape(hid_shape), "dp", axis=1, tiled=True),
        lax.all_gather(results[1], "dp", axis=1, tiled=True),
    )
    x_cols = flat_rows(columns[0])
    g_cols = flat_rows(columns[1])
    gate_grad = jnp.einsum(
        "jrd,jrf->jdf", x_cols, flat_rows(hiddens[0]), preferred_element_type=f32
    ).astype(bf16)
    up_grad = jnp.einsum(
        "jrd,jrf->jdf", x_cols, flat_rows(hiddens[1]), preferred_element_type=f32
    ).astype(bf16)
    down_grad = jnp.einsum(
        "jrf,jrd->jfd", flat_rows(hiddens[2]), g_cols, preferred_element_type=f32
    ).astype(bf16)
    return (mixed, token_grad, router_grad, gate_grad, up_grad, down_grad)


def solution(mesh):
    placed = (
        P(("expert", "dp"), None),
        P(("expert", "dp"), None),
        P(),
        P("expert", None, None),
        P("expert", None, None),
        P("expert", None, None),
        P(("expert", "dp"), None),
    )
    return jax.shard_map(
        body,
        mesh=mesh,
        in_specs=placed,
        out_specs=(
            P(("expert", "dp"), None),
            P(("expert", "dp"), None),
            P(),
            P("expert", "dp", None),
            P("expert", "dp", None),
            P("expert", None, "dp"),
        ),
        check_vma=False,
    )
```

profile of v0, /device:TPU:0, one launch (start us, length us, event | category | flops | bytes accessed | tf_op | source)
XLA Modules:
  0.0 935.9 jit_solution(13658574191496700082)
XLA Ops:
  18.7 6.0 gather_fusion
  27.4 59.9 %all_to_all.50 = bf16[2,8,72,2048]{3,2,0,1:T(8,128)(2,1)S(1)} all-to-all(bf16[2,8,72,2048]{3,2,0,1:T(8,128)(2,1)S(1)} %copy_select_fusion), channel_id=1, replica_groups=mesh['expert'=8,'dp'=4] {'expert'}, dimensions={1} | all-to-all | bytes 9437184 | tf_op jit(solution)/shard_map/all_to_all | solution.py:40
  93.6 5.7 multiply_convert_fusion.2
  111.9 7.0 gather_fusion.5
  119.1 5.9 gather_fusion.3
  125.1 40.4 %all-to-all-done.1 = bf16[2,8,72,2048]{3,2,0,1:T(8,128)(2,1)} async-done(((bf16[2,8,72,2048]{3,2,0,1:T(8,128)(2,1)}), bf16[2,8,72,2048]{3,2,0,1:T(8,128)(2,1)}, u32[]{:S(2)}, u32[]{:S(2)}) %all-to-all-start.1) | async-done | bytes 4718624 | tf_op jit(solution)/shard_map/all_to_all | solution.py:53
  170.6 11.8 %gather_fusion.1 = bf16[1024,2048]{1,0:T(8,128)(2,1)} fusion(bf16[1152,2048]{1,0:T(8,128)(2,1)} %bitcast.104, s32[1024]{0:T(1024)S(1)} %broadcast_clamp_fusion), kind=kCustom, calls=%fused_computation.1 | custom fusion | bytes 8392704 | tf_op jit(solution)/shard_map/gather | solution.py:56
  201.3 11.7 %copy.125 = bf16[2,8,72,2048]{2,1,0,3:T(8,128)(2,1)} copy(bf16[2,8,72,2048]{3,2,0,1:T(8,128)(2,1)} %copy-done.3) | data formatting | bytes 9437184 | tf_op jit(solution)/shard_map/all_to_all | solution.py:40
  213.0 43.1 %all-to-all-done.2 = bf16[2,8,72,2048]{3,2,0,1:T(8,128)(2,1)} async-done(((bf16[2,8,72,2048]{3,2,0,1:T(8,128)(2,1)}), bf16[2,8,72,2048]{3,2,0,1:T(8,128)(2,1)}, u32[]{:S(2)}, u32[]{:S(2)}) %all-to-all-start.2) | async-done | bytes 4718624 | tf_op jit(solution)/shard_map/all_to_all | solution.py:62
  266.1 8.5 multiply_convert_fusion
  274.6 11.3 %fusion.34 = f32[2,576,2048]{2,1,0:T(8,128)} fusion(bf16[2,576,640]{2,1,0:T(8,128)(2,1)} %get-tuple-element.11, bf16[2,2048,640]{2,1,0:T(8,128)(2,1)} %param.10), kind=kOutput, calls=%fused_computation.86 | convolution fusion | flops 3019898880 | bytes 16154624 | tf_op jit(solution)/shard_map/jrf,jdf->jrd/dot_general | solution.py:72
  286.0 8.1 add_convert_fusion
  296.5 240.3 %all-to-all-done.4 = bf16[2,8,72,2048]{2,1,0,3:T(8,128)(2,1)} async-done(((bf16[2,8,72,2048]{2,1,0,3:T(8,128)(2,1)}), bf16[2,8,72,2048]{2,1,0,3:T(8,128)(2,1)}, u32[]{:S(2)}, u32[]{:S(2)}) %all-to-all-start.4) | async-done | bytes 4718624 | tf_op jit(solution)/shard_map/all_to_all | solution.py:91
  542.6 11.8 %copy.130 = bf16[2,8,72,2048]{2,1,0,3:T(8,128)(2,1)} copy(bf16[2,8,72,2048]{3,2,0,1:T(8,128)(2,1)} %all-to-all-done.2) | data formatting | bytes 9437184 | tf_op jit(solution)/shard_map/all_to_all | solution.py:62
  554.4 42.3 %all-to-all-done.3 = bf16[2,8,72,2048]{3,2,0,1:T(8,128)(2,1)} async-done(((bf16[2,8,72,2048]{3,2,0,1:T(8,128)(2,1)}), bf16[2,8,72,2048]{3,2,0,1:T(8,128)(2,1)}, u32[]{:S(2)}, u32[]{:S(2)}) %all-to-all-start.3) | async-done | bytes 4718624 | tf_op jit(solution)/shard_map/all_to_all | solution.py:76
  596.7 5.6 all-to-all-start.5
  608.9 10.7 %copy.142 = bf16[2,8,72,4,512]{4,3,2,1,0:T(4,128)(2,1)} copy(bf16[2,8,72,4,512]{2,1,0,4,3:T(8,128)(2,1)} %bitcast.23) | data formatting | bytes 9437184 | tf_op jit(solution)/shard_map/all_to_all | solution.py:91
  630.4 11.8 %gather_fusion.4 = bf16[1024,2048]{1,0:T(8,128)(2,1)} fusion(bf16[1152,2048]{1,0:T(8,128)(2,1)} %bitcast.103, s32[1024]{0:T(1024)S(1)} %broadcast_clamp_fusion), kind=kCustom, calls=%fused_computation.4 | custom fusion | bytes 8392704 | tf_op jit(solution)/shard_map/gather | solution.py:79
  648.3 184.7 %all-to-all-done.5 = bf16[2,8,72,2048]{2,1,0,3:T(8,128)(2,1)} async-done(((bf16[2,8,72,2048]{2,1,0,3:T(8,128)(2,1)}), bf16[2,8,72,2048]{2,1,0,3:T(8,128)(2,1)}, u32[]{:S(2)}, u32[]{:S(2)}) %all-to-all-start.5) | async-done | bytes 4718624 | tf_op jit(solution)/shard_map/all_to_all | solution.py:92
  833.0 13.2 %copy.131 = bf16[2,8,72,4,512]{4,2,1,3,0:T(8,128)(2,1)} copy(bf16[2,8,72,4,512]{2,1,0,4,3:T(8,128)(2,1)} %bitcast.32) | data formatting | bytes 9437184 | tf_op jit(solution)/shard_map/all_to_all | solution.py:92
  846.3 8.4 convolution_convert_fusion.1
  854.7 9.1 convolution_convert_fusion.3
  863.8 9.2 convolution_convert_fusion.2
  873.0 54.0 %all-reduce.2.cloned.1.call-done = f32[2048,16]{0,1:T(8,128)} async-done(((f32[2048,16]{0,1:T(8,128)}), f32[2048,16]{0,1:T(8,128)}) %all-reduce.2.cloned.1.call-update) | async-done | bytes 131088 | tf_op jit(solution)/shard_map/psum | solution.py:85
  (114 shorter events, 99.6 us)
Async XLA Ops:
  8.0 111.1 %copy-start = (bf16[128,2048]{1,0:T(8,128)(2,1)S(1)}, bf16[128,2048]{1,0:T(8,128)(2,1)}, u32[]{:S(2)}) copy-start(bf16[128,2048]{1,0:T(8,128)(2,1)} %param.13) | copy-start | bytes 1572868
  8.0 10.7 %copy-start.2 = (bf16[128,2048]{1,0:T(8,128)(2,1)S(1)}, bf16[128,2048]{1,0:T(8,128)(2,1)}, u32[]{:S(2)}) copy-start(bf16[128,2048]{1,0:T(8,128)(2,1)} %param.7) | copy-start | bytes 1572868
  8.9 15.8 %copy-start.6 = (s32[128,8]{1,0:T(8,128)}, s32[128,8]{1,0:T(8,128)S(1)}, u32[]{:S(2)}) copy-start(s32[128,8]{1,0:T(8,128)S(1)} %copy.108) | copy-start | bytes 12292
  27.4 62.3 %slice-start.2 = ((s8[5242880]{0:T(1024)(128)(4,1)}), s8[4194304]{0:T(1024)(128)(4,1)S(1)}, s32[]{:S(2)}) async-start(s8[5242880]{0:T(1024)(128)(4,1)} %bitcast.133), calls=%async_computation.12 | async-start | bytes 8388608
  87.3 6.3 slice-start.4
  89.7 9.6 %slice-start = ((s8[5242880]{0:T(1024)(128)(4,1)}), s8[4194304]{0:T(1024)(128)(4,1)S(1)}, s32[]{:S(2)}) async-start(s8[5242880]{0:T(1024)(128)(4,1)} %bitcast.131), calls=%async_computation.10 | async-start | bytes 8388608
  93.6 5.7 copy-start.10
  93.6 5.7 slice-start.1
  99.3 4.1 copy-start.4
  106.0 5.5 copy-start.9
  106.0 5.7 copy-start.8
  106.0 59.5 %all-to-all-start.1 = ((bf16[2,8,72,2048]{3,2,0,1:T(8,128)(2,1)}), bf16[2,8,72,2048]{3,2,0,1:T(8,128)(2,1)}, u32[]{:S(2)}, u32[]{:S(2)}) async-start(bf16[2,8,72,2048]{3,2,0,1:T(8,128)(2,1)} %copy.116), calls=%async_computation.1 | async-start | bytes 9437184 | tf_op jit(solution)/shard_map/all_to_all | solution.py:53
  110.7 735.6 %all-gather.8.cloned.1.call-start = ((), (), s32[]{:S(2)}) async-start(), calls=%async_computation.9 | async-start | bytes 7372800 | tf_op jit(solution)/shard_map/all_gather | solution.py:98
  196.7 59.4 %all-to-all-start.2 = ((bf16[2,8,72,2048]{3,2,0,1:T(8,128)(2,1)}), bf16[2,8,72,2048]{3,2,0,1:T(8,128)(2,1)}, u32[]{:S(2)}, u32[]{:S(2)}) async-start(bf16[2,8,72,2048]{3,2,0,1:T(8,128)(2,1)} %fusion.1), calls=%async_computation.2 | async-start | bytes 9437184 | tf_op jit(solution)/shard_map/all_to_all | solution.py:62
  256.1 280.8 %all-to-all-start.4 = ((bf16[2,8,72,2048]{2,1,0,3:T(8,128)(2,1)}), bf16[2,8,72,2048]{2,1,0,3:T(8,128)(2,1)}, u32[]{:S(2)}, u32[]{:S(2)}) async-start(bf16[2,8,72,2048]{2,1,0,3:T(8,128)(2,1)} %copy.125), calls=%async_computation.4 | async-start | bytes 16777216 | tf_op jit(solution)/shard_map/all_to_all | solution.py:91
  261.7 593.1 %all-gather.4.cloned.1.call-start = ((), (), s32[]{:S(2)}) async-start(), calls=%async_computation.7 | async-start | bytes 7372800 | tf_op jit(solution)/shard_map/all_gather | solution.py:96
  262.0 4.1 copy-start.12
  274.6 11.3 %copy-start.5 = (bf16[2,576,640]{2,1,0:T(8,128)(2,1)}, bf16[2,576,640]{2,1,0:T(8,128)(2,1)S(1)}, u32[]{:S(2)}) copy-start(bf16[2,576,640]{2,1,0:T(8,128)(2,1)S(1)} %get-tuple-element.10) | copy-start | bytes 4423684
  536.9 59.8 %all-to-all-start.3 = ((bf16[2,8,72,2048]{3,2,0,1:T(8,128)(2,1)}), bf16[2,8,72,2048]{3,2,0,1:T(8,128)(2,1)}, u32[]{:S(2)}, u32[]{:S(2)}) async-start(bf16[2,8,72,2048]{3,2,0,1:T(8,128)(2,1)} %copy.122), calls=%async_computation.3 | async-start | bytes 9437184 | tf_op jit(solution)/shard_map/all_to_all | solution.py:76
  541.8 322.0 %all-gather.6.cloned.1.call-start = ((), (), s32[]{:S(2)}) async-start(), calls=%async_computation.8 | async-start | bytes 7372800 | tf_op jit(solution)/shard_map/all_gather | solution.py:97
  596.7 236.3 %all-to-all-start.5 = ((bf16[2,8,72,2048]{2,1,0,3:T(8,128)(2,1)}), bf16[2,8,72,2048]{2,1,0,3:T(8,128)(2,1)}, u32[]{:S(2)}, u32[]{:S(2)}) async-start(bf16[2,8,72,2048]{2,1,0,3:T(8,128)(2,1)} %copy.130), calls=%async_computation.5 | async-start | bytes 16777216 | tf_op jit(solution)/shard_map/all_to_all | solution.py:92
  602.3 5.3 copy-start.7
  602.3 324.6 %all-reduce.2.cloned.1.call-start = ((), (), s32[]{:S(2)}) async-start(), calls=%async_computation.6 | async-start | bytes 262144 | tf_op jit(solution)/shard_map/psum | solution.py:85
  863.8 64.7 %copy-start.1 = (bf16[128,2048]{1,0:T(8,128)(2,1)S(1)}, bf16[128,2048]{1,0:T(8,128)(2,1)}, u32[]{:S(2)}) copy-start(bf16[128,2048]{1,0:T(8,128)(2,1)} %param.13) | copy-start | bytes 1572868
  (4 other events, 11.9 us)
Sparse Core Ops, SparseCore 0:
  113.1 110.4 all-gather.7
  274.8 220.9 all-gather.3
  544.3 178.8 all-gather.5
Sparse Core Ops, SparseCore 1:
  609.0 317.9 all-reduce.1
where the time goes:
time: 946 us; the launch traced here: 936 us
  waiting for transfers between devices  606 us (64%)
  local copies, waits for them, and re-layouts  132 us (14%)
  matrix products  79 us (8%)
  blocking collectives  59.9 us (6%)
  starting transfers between devices  26.6 us (3%)
  other arithmetic  17 us (2%)
  between operations  15.8 us (2%)
    all_to_all x1, waiting for transfers between devices, body(): lax.all_to_all(arrived4, 'dp', split_axis=3, concat_axis=1, tiled=True)  240 us
    all_to_all x1, waiting for transfers between devices, body(): lax.all_to_all(grad_in4, 'dp', split_axis=3, concat_axis=1, tiled=True)  185 us
    all_to_all x1, blocking collectives, body(): lax.all_to_all(send, 'expert', split_axis=1, concat_axis=1, tiled=True)  59.9 us
    psum x1, waiting for transfers between devices, body(): lax.psum(jnp.dot(tokens.T, logit_grad, preferred_element_type=f32), ('exp...  54 us
    all_to_all x1, waiting for transfers between devices, body(): lax.all_to_all(grad_send, 'expert', split_axis=1, concat_axis=1, tiled=True)  43.1 us
    all_to_all x1, waiting for transfers between devices, body(): lax.all_to_all(input_grad, 'expert', split_axis=1, concat_axis=1, tiled=T...  42.3 us
    all_to_all x1, waiting for transfers between devices, body(): lax.all_to_all(expert_out, 'expert', split_axis=1, concat_axis=1, tiled=T...  40.4 us
  transfers between devices with their start and end apart: 9, of which 6 were waited for; matrix products, arithmetic and copies ran while one was open for 20% of the time, Pallas kernels for 0%

commit v1 on v0

--- a/solution.py
+++ b/solution.py
@@ -1,14 +1,327 @@
+import functools
+
 import jax
 import jax.numpy as jnp
 from jax import lax
+from jax.experimental import pallas as pl
+from jax.experimental.pallas import tpu as pltpu
 from jax.sharding import PartitionSpec as P
+
+F32 = jnp.float32
+BF16 = jnp.bfloat16
+LANES = 128
+PLANE = 8
+
+
+def mm(a, b, contract):
+    return lax.dot_general(a, b, (contract, ((), ())), preferred_element_type=F32)
+
+
+NN = ((1,), (0,))
+NT = ((1,), (1,))
+TN = ((0,), (0,))
+
+
+def expert_kernel(own, last, tok, width, ff, cols, units, *refs):
+    refs = list(refs)
+    scal = refs.pop(0)
+    blocks = [refs.pop(0) for _ in units]
+    wc, wd = refs.pop(0), refs.pop(0)
+    acc_in = None if own else refs.pop(0)
+    outs = [refs.pop(0) for _ in range(3 if last else 1)]
+    if own:
+        hid, gu, rp_out = (refs.pop(0) for _ in range(3))
+    x_s, o_s, wc_s, wd_s, pre_s, q_s, gb, acc_s = (refs.pop(0) for _ in range(8))
+    if own:
+        a_s, sacc = refs.pop(0), refs.pop(0)
+    else:
+        hid, gu = refs.pop(0), refs.pop(0)
+    sems = refs.pop(0)
+    rows = PLANE * tok
+    both = 2 * ff
+    chunk_rows = pre_s.shape[0]
+    first_expert = scal[0]
+    zcol = pl.multiple_of(scal[1] * cols, LANES)
+    tiles_e = ff // LANES
+
+    taken = iter(range(64))
+    x_copies, o_copies = [], []
+    place = 2
+    for ref, count in zip(blocks, units):
+        for u in range(count):
+            at = pl.ds(pl.multiple_of(scal[place] * tok, tok), tok)
+            place += 1
+            base = 2 * tok * u
+            x_copies.append(
+                pltpu.make_async_copy(ref.at[pl.ds(base, tok), :], x_s.at[at, :], sems.at[next(taken)])
+            )
+            o_copies.append(
+                pltpu.make_async_copy(
+                    ref.at[pl.ds(base + tok, tok), pl.ds(0, width)], o_s.at[at, :], sems.at[next(taken)]
+                )
+            )
+
+    def part(src, dst, lo, size):
+        return pltpu.make_async_copy(
+            src.at[:, pl.ds(lo, size)], dst.at[:, pl.ds(lo, size)], sems.at[next(taken)]
+        )
+
+    gate_copy = part(wc, wc_s, 0, both)
+    up_copy = part(wc, wc_s, both, both + LANES)
+    wd_copy = pltpu.make_async_copy(wd, wd_s, sems.at[next(taken)])
+    acc_copies = []
+    if not own:
+        acc_copies = [pltpu.make_async_copy(acc_in, acc_s, sems.at[next(taken)])]
+    for copy in [*x_copies, gate_copy, up_copy, *o_copies, wd_copy, *acc_copies]:
+        copy.start()
+    out_sem = next(taken)
+    for copy in [*x_copies, gate_copy, up_copy]:
+        copy.wait()
+
+    lane = lax.broadcasted_iota(jnp.int32, (chunk_rows, LANES), 1)
+
+    def chunk(c, carry):
+        here = pl.ds(pl.multiple_of(c * chunk_rows, chunk_rows), chunk_rows)
+        pre_s[...] = mm(x_s[here, :width], wc_s[...], NN)
+
+        @pl.when(c == 0)
+        def _():
+            for copy in [*o_copies, wd_copy]:
+                copy.wait()
+
+        q_s[...] = mm(o_s[here, :], wd_s[...], NT)
+        score = jax.nn.sigmoid(pre_s[:, 2 * both :])
+        chosen = score * x_s[here, width:].astype(F32)
+        gates = chosen / jnp.sum(chosen, axis=1, keepdims=True)
+        for j in range(2):
+            col = jnp.sum(jnp.where(lane == first_expert + j, gates, 0.0), axis=1, keepdims=True)
+            gb[j, here, :] = jnp.broadcast_to(col, (chunk_rows, LANES))
+        if own:
+            a_s[here, :] = gates * (1.0 - score)
+            sacc[:, here, :] = jnp.zeros((2, chunk_rows, LANES), F32)
+
+        def piece(i, carry):
+            r = pl.ds(pl.multiple_of(i * LANES, LANES), LANES)
+            ra = pl.ds(pl.multiple_of(c * chunk_rows + i * LANES, LANES), LANES)
+            for t in range(both // LANES):
+                expert = t // tiles_e
+                gate = gb[expert, ra, :]
+                pre = pre_s[r, t * LANES : (t + 1) * LANES]
+                up = pre_s[r, both + t * LANES : both + (t + 1) * LANES]
+                q = q_s[r, t * LANES : (t + 1) * LANES]
+                sig = 0.5 * jnp.tanh(0.5 * pre) + 0.5
+                silu = pre * sig
+                h = silu * up
+                gq = gate * q
+                hid[ra, t * LANES : (t + 1) * LANES] = (gate * h).astype(BF16)
+                gu[ra, t * LANES : (t + 1) * LANES] = (gq * up * (sig + silu * (1.0 - sig))).astype(BF16)
+                gu[ra, both + t * LANES : both + (t + 1) * LANES] = (gq * silu).astype(BF16)
+                if own:
+                    sacc[expert, ra, :] += h * q
+            return carry
+
+        lax.fori_loop(0, chunk_rows // LANES, piece, 0)
+        return carry
+
+    lax.fori_loop(0, rows // chunk_rows, chunk, 0)
+
+    for copy in acc_copies:
+        copy.wait()
+    def weight_grad(i, grad):
+        if not own:
+            grad = grad + acc_s[i]
+        acc_s[i] = grad
+        if not last:
+            pltpu.make_async_copy(acc_s.at[i], outs[0].at[i], sems.at[out_sem + i]).start()
+
+    def from_tokens(i, carry):
+        part = pl.ds(pl.multiple_of(i * both, LANES), both)
+        weight_grad(i, mm(x_s[:, pl.ds(zcol, cols)], gu[:, part], TN))
+        return carry
+
+    lax.fori_loop(0, 2, from_tokens, 0)
+    weight_grad(2, mm(o_s[:, pl.ds(zcol, cols)], hid[...], TN))
+    if last:
+        for i in range(2):
+            for e in range(2):
+                outs[i][e] = acc_s[i, :, e * ff : (e + 1) * ff].astype(BF16)
+        for e in range(2):
+            outs[2][e] = acc_s[2, :, e * ff : (e + 1) * ff].T.astype(BF16)
+
+    if own:
+        lane = lax.broadcasted_iota(jnp.int32, (rows, LANES), 1)
+        term = jnp.zeros((rows, LANES), F32)
+        shared = jnp.zeros((rows, LANES), F32)
+        for j in range(2):
+            sens = jnp.sum(sacc[j], axis=1, keepdims=True)
+            term = term + jnp.where(lane == first_expert + j, sens, 0.0)
+            shared = shared + gb[j] * sens
+        grad = a_s[...] * (term - shared)
+        high = grad.astype(BF16)
+        low = (grad - high.astype(F32)).astype(BF16)
+        gu[:, 2 * both : 2 * both + LANES] = high
+        gu[:, 2 * both + LANES :] = low
+        n_out = rp_out.shape[0]
+        split = gu[:, 2 * both :]
+        terms = mm(split, x_s[:, :width], TN)
+        rp_out[...] = terms[:n_out] + terms[LANES : LANES + n_out]
+    if not last:
+        for i in range(3):
+            pltpu.make_async_copy(acc_s.at[i], outs[0].at[i], sems.at[out_sem + i]).wait()
+
+
+def expert_call(own, last, scal, blocks, wc, wd, acc, n_experts):
+    tok = sum(b.shape[0] for b in blocks) // (2 * PLANE)
+    units = tuple(b.shape[0] // (2 * tok) for b in blocks)
+    both, width = wd.shape
+    ff = both // 2
+    cols = width // lax.axis_size("dp")
+    rows = PLANE * tok
+    anywhere = pl.BlockSpec(memory_space=pl.ANY)
+    vmem = pl.BlockSpec(memory_space=pltpu.VMEM)
+    args = [*blocks, wc, wd]
+    if not own:
+        args.append(acc)
+    if last:
+        out_shape = [jax.ShapeDtypeStruct((2, cols, ff), BF16)] * 2 + [jax.ShapeDtypeStruct((2, ff, cols), BF16)]
+        out_specs = [vmem] * 3
+    else:
+        out_shape = [jax.ShapeDtypeStruct((3, cols, both), F32)]
+        out_specs = [anywhere]
+    if own:
+        out_shape += [
+            jax.ShapeDtypeStruct((rows, both), BF16),
+            jax.ShapeDtypeStruct((rows, 2 * both + 2 * LANES), BF16),
+            jax.ShapeDtypeStruct((n_experts, width), F32),
+        ]
+        out_specs += [vmem] * 3
+    chunk = rows // 4
+    scratch = [
+        pltpu.VMEM((rows, width + LANES), BF16),
+        pltpu.VMEM((rows, width), BF16),
+        pltpu.VMEM((width, 2 * both + LANES), BF16),
+        pltpu.VMEM((both, width), BF16),
+        pltpu.VMEM((chunk, 2 * both + LANES), F32),
+        pltpu.VMEM((chunk, both), F32),
+        pltpu.VMEM((2, rows, LANES), F32),
+        pltpu.VMEM((3, cols, both), F32),
+    ]
+    if own:
+        scratch += [pltpu.VMEM((rows, LANES), F32), pltpu.VMEM((2, rows, LANES), F32)]
+    else:
+        scratch += [pltpu.VMEM((rows, both), BF16), pltpu.VMEM((rows, 2 * both), BF16)]
+    scratch.append(pltpu.SemaphoreType.DMA((2 * PLANE + 7,)))
+    aliases = {} if own or last else {1 + len(blocks) + 2: 0}
+    flops = 2 * rows * width * both * 3 + 2 * rows * cols * both * 3
+    return pl.pallas_call(
+        functools.partial(expert_kernel, own, last, tok, width, ff, cols, units),
+        grid_spec=pltpu.PrefetchScalarGridSpec(
+            num_scalar_prefetch=1,
+            grid=(),
+            in_specs=[anywhere] * len(args),
+            out_specs=out_specs,
+            scratch_shapes=scratch,
+        ),
+        out_shape=out_shape,
+        input_output_aliases=aliases,
+        compiler_params=pltpu.CompilerParams(vmem_limit_bytes=58 * 1024 * 1024),
+        cost_estimate=pl.CostEstimate(flops=flops, bytes_accessed=40_000_000, transcendentals=rows * both),
+        name="experts_own" if own else "experts_last" if last else "experts_mid",
+    )(scal, *args)
+
+
+def flip(x, even, odd):
+    groups = lax.axis_size("expert")
+    return lax.ppermute(x, "expert", [(i, i ^ (odd if i % 2 else even)) for i in range(groups)])
+
+
+def dense_body(tokens, expert_ids, router, w_gate, w_up, w_down, out_grad):
+    tok, width = tokens.shape
+    n_experts = router.shape[1]
+    ff = w_gate.shape[2]
+    n_dp = lax.axis_size("dp")
+    me = lax.axis_index("expert")
+    core = me % 2
+    ladder = jnp.arange(LANES, dtype=jnp.int32)
+    mask = jnp.any(expert_ids[:, :, None] == ladder[None, None, :], axis=1).astype(BF16)
+    block = jnp.concatenate(
+        [
+            jnp.concatenate([tokens, mask], axis=1),
+            jnp.concatenate([out_grad, jnp.zeros((tok, LANES), BF16)], axis=1),
+        ],
+        axis=0,
+    )
+    router_pad = jnp.pad(router, ((0, 0), (0, LANES - n_experts)))
+    wc = jnp.concatenate([w_gate[0], w_gate[1], w_up[0], w_up[1], router_pad, router_pad], axis=1)
+    wd = w_down.reshape(2 * ff, width)
+    near_at = me ^ jnp.where(core == 0, 2, 4)
+    other_at = me ^ jnp.where(core == 0, 5, 3)
+    scal = jnp.stack(
+        [me * 2, lax.axis_index("dp"), me, me ^ 1, near_at, near_at ^ 1, other_at, other_at ^ 1, me ^ 6, me ^ 7]
+    ).astype(jnp.int32)
+    ring = [(i, (i + 1) % n_dp) for i in range(n_dp)]
+
+    def pair_of(b):
+        return jnp.concatenate([b, flip(b, 1, 1)], axis=0)
+
+    half = 2 * tok
+    alone, pairs, nears, others, diagonals = ({} for _ in range(5))
+    alone[0] = block
+    alone[1] = lax.ppermute(block, "dp", ring)
+    pairs[0] = pair_of(block)
+    nears[0] = flip(pairs[0], 2, 4)
+    pairs[1] = pair_of(alone[1])
+    acc = None
+    for g in range(-1, n_dp):
+        if g + 1 < n_dp:
+            diagonals[g + 1] = flip(nears[g + 1][:half], 4, 2)
+            others[g + 1] = flip(nears[g + 1], 1, 1)
+        if g + 2 < n_dp:
+            nears[g + 2] = flip(pairs[g + 2], 2, 4)
+        if g + 3 < n_dp:
+            alone[g + 3] = lax.ppermute(alone[g + 2], "dp", ring)
+        if g == 1:
+            line = [rp] + [flip(rp, k, k) for k in (2, 4, 6)]
+            part = jnp.dot(hid, wd, preferred_element_type=F32).astype(BF16)
+            mixed = lax.psum_scatter(part, "expert", scatter_dimension=0, tiled=True)
+            part = mm(gu, wc, NT).astype(BF16)
+            token_grad = lax.psum_scatter(part, "expert", scatter_dimension=0, tiled=True)
+        if g == 2:
+            line = [rp] + [lax.ppermute(rp, "dp", [(i, i ^ k) for i in range(n_dp)]) for k in range(1, n_dp)]
+        if g >= 0:
+            out = expert_call(g == 0, g == n_dp - 1, scal, blocks, wc, wd, acc, n_experts)
+            acc = out[0]
+        if g + 1 == n_dp:
+            break
+        if g == 0:
+            hid, gu, rp = out[1:]
+        own_out = (hid, gu, rp) if g == 0 else tuple(line) if g > 0 else ()
+        places = [(d, g + k) for d, k in ((diagonals, 1), (others, 1), (nears, 2), (alone, 3)) if g + k in d]
+        held = list(lax.optimization_barrier((scal if g < 0 else acc, *own_out, *[d[k] for d, k in places])))
+        if g < 0:
+            scal = held.pop(0)
+        else:
+            acc = held.pop(0)
+        own_out = [held.pop(0) for _ in own_out]
+        if g == 0:
+            hid, gu, rp = own_out
+        elif g > 0:
+            rp = (own_out[0] + own_out[1]) + (own_out[2] + own_out[3])
+        for d, k in places:
+            d[k] = held.pop(0)
+        blocks = [pairs[g + 1], nears[g + 1], others[g + 1], diagonals[g + 1], flip(diagonals[g + 1], 1, 1)]
+        if g + 3 < n_dp:
+            pairs[g + 3] = pair_of(alone[g + 3])
+        if g == 0:
+            rp = rp + flip(rp, 1, 1)
+    return (mixed, token_grad, rp.T, *out)
 
 
 def flat_rows(array):
     return array.reshape(array.shape[0], array.shape[1] * array.shape[2], array.shape[3])
 
 
-def body(tokens, expert_ids, router, w_gate, w_up, w_down, out_grad):
+def sparse_body(tokens, expert_ids, router, w_gate, w_up, w_down, out_grad):
     f32 = jnp.float32
     bf16 = jnp.bfloat16
     tok_dev, width = tokens.shape
@@ -111,6 +424,12 @@
     return (mixed, token_grad, router_grad, gate_grad, up_grad, down_grad)
 
 
+def body(*args):
+    plane = lax.axis_size("expert") == 8 and args[3].shape[0] == 2
+    line = lax.axis_size("dp")
+    return (dense_body if plane and line == 4 else sparse_body)(*args)
+
+
 def solution(mesh):
     placed = (
         P(("expert", "dp"), None),

time: 946 us -> 316 us (0.33)
  waiting for transfers between devices: 606 us -> 56 us
  Pallas kernels: 0 us -> 154 us
  local copies, waits for them, and re-layouts: 132 us -> 30.7 us
  blocking collectives: 59.9 us -> 0 us
  matrix products: 79 us -> 28.4 us
  other arithmetic: 17 us -> 3.49 us
    all_to_all x5 -> x0, waiting for transfers between devices: 551 us -> none  [the longest x1 240 us: body(): lax.all_to_all(arrived4, 'dp', split_axis=3, concat_axis=1, tiled=True)]
    pallas_call x0 -> x4, Pallas kernels: none -> 154 us  [expert_call(): pl.pallas_call(functools.partial(expert_kernel, own, last, tok, width, ff...]
    all_to_all x9 -> x0, local copies, waits for them, and re-layouts: 67 us -> none  [the longest x2 16.2 us: body(): lax.all_to_all(arrived4, 'dp', split_axis=3, concat_axis=1, tiled=True)]
    all_to_all x1 -> x0, blocking collectives: 59.9 us -> none  [body(): lax.all_to_all(send, 'expert', split_axis=1, concat_axis=1, tiled=True)]
    ppermute x0 -> x30, waiting for transfers between devices: none -> 56 us  [the longest x1 24.3 us: dense_body(): alone[1] = lax.ppermute(block, 'dp', ring)]
    psum x1 -> x0, waiting for transfers between devices: 54 us -> none  [body(): lax.psum(jnp.dot(tokens.T, logit_grad, preferred_element_type=f32), ('exp...]
    dot_general x15 -> x2, matrix products: 79 us -> 28.4 us  [the longest x1 18.3 us: mm(): lax.dot_general(a, b, (contract, ((), ())), preferred_element_type=F32)]
    gather x10 -> x0, local copies, waits for them, and re-layouts: 47.4 us -> none  [the longest x1 11.8 us: body(): picked = back[dest].reshape(tok_dev, top, width)]
  transfers between devices with their start and end apart: 9 -> 32, of which waited for: 6 -> 7; matrix products, arithmetic and copies ran while one was open for 20% -> 15% of each run, Pallas kernels for 0% -> 49%
where the time goes in v1:
time: 316 us; the launch traced here: 312 us
  Pallas kernels  154 us (49%)
  waiting for transfers between devices  56 us (18%)
  local copies, waits for them, and re-layouts  30.7 us (10%)
  matrix products  28.4 us (9%)
  starting transfers between devices  25 us (8%)
  between operations  14.6 us (5%)
  other arithmetic  3.49 us (1%)
    pallas_call x4, Pallas kernels, expert_call(): pl.pallas_call(functools.partial(expert_kernel, own, last, tok, width, ff...  154 us
    ppermute x1, waiting for transfers between devices, dense_body(): alone[1] = lax.ppermute(block, 'dp', ring)  24.3 us
    unnamed x36, local copies, waits for them, and re-layouts  20.4 us
    ppermute x2, waiting for transfers between devices, dense_body(): alone[g + 3] = lax.ppermute(alone[g + 2], 'dp', ring)  18.7 us
    dot_general x1, matrix products, mm(): lax.dot_general(a, b, (contract, ((), ())), preferred_element_type=F32)  18.3 us
    ppermute x24, starting transfers between devices, flip(): lax.ppermute(x, 'expert', [(i, i ^ (odd if i % 2 else even)) for i in ran...  17.4 us
    ppermute x24, waiting for transfers between devices, flip(): lax.ppermute(x, 'expert', [(i, i ^ (odd if i % 2 else even)) for i in ran...  12.9 us
    dot_general x1, matrix products, dense_body(): part = jnp.dot(hid, wd, preferred_element_type=F32).astype(BF16)  10.1 us
  transfers between devices with their start and end apart: 32, of which 7 were waited for; matrix products, arithmetic and copies ran while one was open for 15% of the time, Pallas kernels for 49%

profile of v1, /device:TPU:0, one launch (start us, length us, event | category | flops | bytes accessed | tf_op | source)
XLA Modules:
  0.0 311.8 jit_solution(1784239947632947895)
XLA Ops:
  11.1 2.6 collective-permute-start.4
  13.9 2.7 collective-permute-start.1
  16.6 24.3 %collective-permute-done.4 = bf16[256,2176]{1,0:T(8,128)(2,1)S(1)} collective-permute-done((bf16[256,2176]{1,0:T(8,128)(2,1)S(1)}, bf16[256,2176]{1,0:T(8,128)(2,1)S(1)}, u32[]{:S(2)}, u32[]{:S(2)}) %collective-permute-start.4) | collective-permute-done | bytes 1114144 | tf_op jit(solution)/shard_map/ppermute | solution.py:270
  42.1 1.6 collective-permute-done.5
  44.7 1.5 collective-permute-start.6
  48.4 1.6 collective-permute-start.2
  50.0 3.5 %bitcast_dynamic-update-slice_fusion.3 = bf16[2048,2816]{1,0:T(8,128)(2,1)} fusion(bf16[2,2048,640]{2,1,0:T(8,128)(2,1)} %param.10), kind=kLoop, calls=%fused_computation.5 | loop fusion | bytes 5242880
  53.6 3.6 %bitcast_dynamic-update-slice_fusion.2 = bf16[2048,2816]{1,0:T(8,128)(2,1)} fusion(bf16[2048,2816]{1,0:T(8,128)(2,1)} %bitcast_dynamic-update-slice_fusion.3, bf16[2,2048,640]{2,1,0:T(8,128)(2,1)} %param.10), kind=kLoop, calls=%fused_computation.4 | loop fusion | bytes 5242880
  57.2 18.7 %collective-permute-done.7 = bf16[256,2176]{1,0:T(8,128)(2,1)S(1)} collective-permute-done((bf16[256,2176]{1,0:T(8,128)(2,1)}, bf16[256,2176]{1,0:T(8,128)(2,1)S(1)}, u32[]{:S(2)}, u32[]{:S(2)}) %collective-permute-start.7) | collective-permute-done | bytes 1114144 | tf_op jit(solution)/shard_map/ppermute | solution.py:282
  76.0 8.4 %collective-permute-done.6.refs_2_ = bf16[512,2176]{1,0:T(8,128)(2,1)} collective-permute-done((bf16[512,2176]{1,0:T(8,128)(2,1)}, bf16[512,2176]{1,0:T(8,128)(2,1)}, u32[]{:S(2)}, u32[]{:S(2)}) %collective-permute-start.6) | collective-permute-done | bytes 2228256 | tf_op jit(solution)/shard_map/ppermute | solution.py:235
  84.5 1.8 bitcast_dynamic-update-slice_fusion.1
  86.5 3.6 %bitcast_dynamic-update-slice_fusion = bf16[2048,2816]{1,0:T(8,128)(2,1)} fusion(bf16[2048,2816]{1,0:T(8,128)(2,1)} %bitcast_dynamic-update-slice_fusion.1, bf16[2,2048,640]{2,1,0:T(8,128)(2,1)} %param.11), kind=kLoop, calls=%fused_computation.2 | loop fusion | bytes 5242880
  92.8 1.5 collective-permute-start.12
  97.8 1.6 collective-permute-start.9
  100.4 41.2 %experts_own.1 = (f32[3,512,1280]{2,1,0:T(8,128)}, bf16[1024,1280]{1,0:T(8,128)(2,1)}, bf16[1024,2816]{1,0:T(8,128)(2,1)}, f32[16,2048]{1,0:T(8,128)}) custom-call(s32[10]{0:T(128)} %stack.43.refs_0_, bf16[512,2176]{1,0:T(8,128)(2,1)} %copy-done, bf16[512,2176]{1,0:T(8,128)(2,1)} %collective-permute-done.1.refs_2_, ...), custom_call_target="tpu_custom_call" | custom-call | flops 20132659200 | bytes 40000000 | tf_op jit(solution)/shard_map/experts_own/pallas_call | solution.py:216
  141.7 10.1 %convolution_convert_fusion.1 = bf16[1024,2048]{1,0:T(8,128)(2,1)} fusion(bf16[1024,1280]{1,0:T(8,128)(2,1)} %get-tuple-element.50, bf16[1280,2048]{1,0:T(8,128)(2,1)} %bitcast.28), kind=kOutput, calls=%fused_computation.1 | convolution fusion | flops 5370806272 | bytes 12058624 | tf_op jit(solution)/shard_map/dot_general | solution.py:285
  156.8 1.5 collective-permute-start.22
  158.3 18.3 %convolution_convert_fusion = bf16[1024,2048]{1,0:T(8,128)(2,1)} fusion(bf16[1024,2816]{1,0:T(8,128)(2,1)} %get-tuple-element.51, bf16[2048,2816]{1,0:T(8,128)(2,1)} %pad_dynamic-update-slice_fusion.1.refs_6_), kind=kOutput, calls=%fused_computation | convolution fusion | flops 11813257216 | bytes 21495808 | tf_op jit(solution)/shard_map/dot_general | solution.py:17
  178.6 1.5 collective-permute-start.17
  181.3 36.7 %experts_mid.2.refs_8_ = f32[3,512,1280]{2,1,0:T(8,128)} custom-call(s32[10]{0:T(128)} %stack.43.refs_0_, bf16[512,2176]{1,0:T(8,128)(2,1)} %constant_dynamic-update-slice_fusion.refs_1_, bf16[512,2176]{1,0:T(8,128)(2,1)} %collective-permute-done.6.refs_2_, bf16[512,2176]{1,0:T(8,128)(2,1)} %collective-permute-done.10.refs_3_, ...), custom_call_target="tpu_custom_call", output_to_operand_aliasing={{}: (8, {})} | custom-call | flops 20132659200 | bytes 40000000 | tf_op jit(solution)/shard_map/experts_mid/pallas_call | solution.py:216
  221.2 2.6 collective-permute-start.25
  225.2 37.7 %experts_mid.3.refs_8_ = f32[3,512,1280]{2,1,0:T(8,128)} custom-call(s32[10]{0:T(128)} %stack.43.refs_0_, bf16[512,2176]{1,0:T(8,128)(2,1)} %constant_dynamic-update-slice_fusion.2.refs_1_, bf16[512,2176]{1,0:T(8,128)(2,1)} %collective-permute-done.12.refs_2_, bf16[512,2176]{1,0:T(8,128)(2,1)} %collective-permute-done.20.refs_3_, ...), custom_call_target="tpu_custom_call", output_to_operand_aliasing={{}: (8, {})} | custom-call | flops 20132659200 | bytes 40000000 | tf_op jit(solution)/shard_map/experts_mid/pallas_call | solution.py:216
  264.0 1.9 collective-permute-done.29.refs_5_
  266.9 37.8 %experts_last.1 = (bf16[2,512,640]{2,1,0:T(8,128)(2,1)}, bf16[2,512,640]{2,1,0:T(8,128)(2,1)}, bf16[2,640,512]{2,1,0:T(8,128)(2,1)}) custom-call(s32[10]{0:T(128)} %stack.43.refs_0_, bf16[512,2176]{1,0:T(8,128)(2,1)} %constant_dynamic-update-slice_fusion.4.refs_1_, bf16[512,2176]{1,0:T(8,128)(2,1)} %copy-done.3, ...), custom_call_target="tpu_custom_call" | custom-call | flops 20132659200 | bytes 40000000 | tf_op jit(solution)/shard_map/experts_last/pallas_call | solution.py:216
  (102 shorter events, 30.7 us)
Async XLA Ops:
  7.2 297.6 %reduce-scatter.3.cloned.1.call-start = ((), (), s32[]{:S(2)}) async-start(), calls=%async_computation.2 | async-start | bytes 4718592 | tf_op jit(solution)/shard_map/reduce_scatter | solution.py:286
  11.1 29.8 %collective-permute-start.4 = (bf16[256,2176]{1,0:T(8,128)(2,1)S(1)}, bf16[256,2176]{1,0:T(8,128)(2,1)S(1)}, u32[]{:S(2)}, u32[]{:S(2)}) collective-permute-start(bf16[256,2176]{1,0:T(8,128)(2,1)S(1)} %pad_maximum_fusion.1), channel_id=1, source_target_pairs={{0,1},{1,2},{2,3},{3,0},{4,5},{5,6},{6,7},{7,4},{8,9},{9,10},{10,1... | collective-permute-start | bytes 3342344 | tf_op jit(solution)/shard_map/ppermute | solution.py:270
  13.9 32.3 %collective-permute-start.1 = (bf16[512,2176]{1,0:T(8,128)(2,1)S(1)}, bf16[512,2176]{1,0:T(8,128)(2,1)}, u32[]{:S(2)}, u32[]{:S(2)}) collective-permute-start(bf16[512,2176]{1,0:T(8,128)(2,1)S(1)} %pad_maximum_fusion.refs_1_), channel_id=1, source_target_pairs={{0,8},{4,20},{8,0},{12,28},{16,24},{20,4},{24,16},{28,12},{1,9},{5... | collective-permute-start | bytes 6684680 | tf_op jit(solution)/shard_map/ppermute | solution.py:235
  44.7 39.7 %collective-permute-start.6 = (bf16[512,2176]{1,0:T(8,128)(2,1)}, bf16[512,2176]{1,0:T(8,128)(2,1)}, u32[]{:S(2)}, u32[]{:S(2)}) collective-permute-start(bf16[512,2176]{1,0:T(8,128)(2,1)} %constant_dynamic-update-slice_fusion.refs_1_), channel_id=1, source_target_pairs={{0,8},{4,20},{8,0},{12,28},{16,24},{20,4},{24,16},{28,12},{1,9},{5... | collective-permute-start | bytes 6684680 | tf_op jit(solution)/shard_map/ppermute | solution.py:235
  46.2 38.2 %collective-permute-start.3 = (bf16[512,2176]{1,0:T(8,128)(2,1)}, bf16[512,2176]{1,0:T(8,128)(2,1)}, u32[]{:S(2)}, u32[]{:S(2)}) collective-permute-start(bf16[512,2176]{1,0:T(8,128)(2,1)} %collective-permute-done.1.refs_2_), channel_id=1, source_target_pairs={{0,4},{4,0},{8,12},{12,8},{16,20},{20,16},{24,28},{28,24},{1,5},{5... | collective-permute-start | bytes 6684680 | tf_op jit(solution)/shard_map/ppermute | solution.py:235
  46.9 29.0 %collective-permute-start.7 = (bf16[256,2176]{1,0:T(8,128)(2,1)}, bf16[256,2176]{1,0:T(8,128)(2,1)S(1)}, u32[]{:S(2)}, u32[]{:S(2)}) collective-permute-start(bf16[256,2176]{1,0:T(8,128)(2,1)} %copy-done.2), channel_id=1, source_target_pairs={{0,1},{1,2},{2,3},{3,0},{4,5},{5,6},{6,7},{7,4},{8,9},{9,10},{10,1... | collective-permute-start | bytes 3342344 | tf_op jit(solution)/shard_map/ppermute | solution.py:282
  48.4 27.6 %collective-permute-start.2 = (bf16[256,2176]{1,0:T(8,128)(2,1)S(1)}, bf16[256,2176]{1,0:T(8,128)(2,1)S(1)}, u32[]{:S(2)}, u32[]{:S(2)}) collective-permute-start(bf16[256,2176]{1,0:T(8,128)(2,1)S(1)} %slice.32), channel_id=1, source_target_pairs={{0,16},{4,12},{8,24},{12,4},{16,0},{20,28},{24,8},{28,20},{1,17},{... | collective-permute-start | bytes 3342344 | tf_op jit(solution)/shard_map/ppermute | solution.py:235
  90.6 51.1 %collective-permute-start.10 = (bf16[512,2176]{1,0:T(8,128)(2,1)}, bf16[512,2176]{1,0:T(8,128)(2,1)}, u32[]{:S(2)}, u32[]{:S(2)}) collective-permute-start(bf16[512,2176]{1,0:T(8,128)(2,1)} %collective-permute-done.6.refs_2_), channel_id=1, source_target_pairs={{0,4},{4,0},{8,12},{12,8},{16,20},{20,16},{24,28},{28,24},{1,5},{5... | collective-permute-start | bytes 6684680 | tf_op jit(solution)/shard_map/ppermute | solution.py:235
  92.8 48.9 %collective-permute-start.12 = (bf16[512,2176]{1,0:T(8,128)(2,1)}, bf16[512,2176]{1,0:T(8,128)(2,1)}, u32[]{:S(2)}, u32[]{:S(2)}) collective-permute-start(bf16[512,2176]{1,0:T(8,128)(2,1)} %constant_dynamic-update-slice_fusion.2.refs_1_), channel_id=1, source_target_pairs={{0,8},{4,20},{8,0},{12,28},{16,24},{20,4},{24,16},{28,12},{1,9},{5... | collective-permute-start | bytes 6684680 | tf_op jit(solution)/shard_map/ppermute | solution.py:235
  97.6 44.1 %collective-permute-start.13 = (bf16[256,2176]{1,0:T(8,128)(2,1)S(1)}, bf16[256,2176]{1,0:T(8,128)(2,1)S(1)}, u32[]{:S(2)}, u32[]{:S(2)}) collective-permute-start(bf16[256,2176]{1,0:T(8,128)(2,1)S(1)} %collective-permute-done.7), channel_id=1, source_target_pairs={{0,1},{1,2},{2,3},{3,0},{4,5},{5,6},{6,7},{7,4},{8,9},{9,10},{10,1... | collective-permute-start | bytes 3342344 | tf_op jit(solution)/shard_map/ppermute | solution.py:282
  97.8 43.8 %collective-permute-start.9 = (bf16[256,2176]{1,0:T(8,128)(2,1)S(1)}, bf16[256,2176]{1,0:T(8,128)(2,1)}, u32[]{:S(2)}, u32[]{:S(2)}) collective-permute-start(bf16[256,2176]{1,0:T(8,128)(2,1)S(1)} %slice.29), channel_id=1, source_target_pairs={{0,16},{4,12},{8,24},{12,4},{16,0},{20,28},{24,8},{28,20},{1,17},{... | collective-permute-start | bytes 3342344 | tf_op jit(solution)/shard_map/ppermute | solution.py:235
  151.8 153.0 %reduce-scatter.5.cloned.1.call-start = ((), (), s32[]{:S(2)}) async-start(), calls=%async_computation.3 | async-start | bytes 4718592 | tf_op jit(solution)/shard_map/reduce_scatter | solution.py:288
  153.8 26.4 %collective-permute-start.14 = (bf16[256,2176]{1,0:T(8,128)(2,1)}, bf16[256,2176]{1,0:T(8,128)(2,1)}, u32[]{:S(2)}, u32[]{:S(2)}) collective-permute-start(bf16[256,2176]{1,0:T(8,128)(2,1)} %collective-permute-done.9.refs_4_), channel_id=1, source_target_pairs={{0,4},{4,0},{8,12},{12,8},{16,20},{20,16},{24,28},{28,24},{1,5},{5... | collective-permute-start | bytes 3342344 | tf_op jit(solution)/shard_map/ppermute | solution.py:235
  154.3 63.8 %collective-permute-start.20 = (bf16[512,2176]{1,0:T(8,128)(2,1)}, bf16[512,2176]{1,0:T(8,128)(2,1)}, u32[]{:S(2)}, u32[]{:S(2)}) collective-permute-start(bf16[512,2176]{1,0:T(8,128)(2,1)} %collective-permute-done.12.refs_2_), channel_id=1, source_target_pairs={{0,4},{4,0},{8,12},{12,8},{16,20},{20,16},{24,28},{28,24},{1,5},{5... | collective-permute-start | bytes 6684680 | tf_op jit(solution)/shard_map/ppermute | solution.py:235
  155.1 23.5 %collective-permute-start.16 = (f32[16,2048]{1,0:T(8,128)S(1)}, f32[16,2048]{1,0:T(8,128)}, u32[]{:S(2)}, u32[]{:S(2)}) collective-permute-start(f32[16,2048]{1,0:T(8,128)S(1)} %add.34), channel_id=1, source_target_pairs={{0,8},{4,12},{8,0},{12,4},{16,24},{20,28},{24,16},{28,20},{1,9},{5... | collective-permute-start | bytes 393224 | tf_op jit(solution)/shard_map/ppermute | solution.py:235
  156.8 61.4 %collective-permute-start.22 = (bf16[512,2176]{1,0:T(8,128)(2,1)}, bf16[512,2176]{1,0:T(8,128)(2,1)S(1)}, u32[]{:S(2)}, u32[]{:S(2)}) collective-permute-start(bf16[512,2176]{1,0:T(8,128)(2,1)} %constant_dynamic-update-slice_fusion.4.refs_1_), channel_id=1, source_target_pairs={{0,8},{4,20},{8,0},{12,28},{16,24},{20,4},{24,16},{28,12},{1,9},{5... | collective-permute-start | bytes 6684680 | tf_op jit(solution)/shard_map/ppermute | solution.py:235
  177.9 40.2 %collective-permute-start.19 = (bf16[256,2176]{1,0:T(8,128)(2,1)S(1)}, bf16[256,2176]{1,0:T(8,128)(2,1)}, u32[]{:S(2)}, u32[]{:S(2)}) collective-permute-start(bf16[256,2176]{1,0:T(8,128)(2,1)S(1)} %slice.30), channel_id=1, source_target_pairs={{0,16},{4,12},{8,24},{12,4},{16,0},{20,28},{24,8},{28,20},{1,17},{... | collective-permute-start | bytes 3342344 | tf_op jit(solution)/shard_map/ppermute | solution.py:235
  178.6 39.5 %collective-permute-start.17 = (f32[16,2048]{1,0:T(8,128)S(1)}, f32[16,2048]{1,0:T(8,128)S(1)}, u32[]{:S(2)}, u32[]{:S(2)}) collective-permute-start(f32[16,2048]{1,0:T(8,128)S(1)} %add.34), channel_id=1, source_target_pairs={{0,16},{4,20},{8,24},{12,28},{16,0},{20,4},{24,8},{28,12},{1,17},{... | collective-permute-start | bytes 393224 | tf_op jit(solution)/shard_map/ppermute | solution.py:235
  180.1 38.0 %collective-permute-start.18 = (f32[16,2048]{1,0:T(8,128)S(1)}, f32[16,2048]{1,0:T(8,128)S(1)}, u32[]{:S(2)}, u32[]{:S(2)}) collective-permute-start(f32[16,2048]{1,0:T(8,128)S(1)} %add.34), channel_id=1, source_target_pairs={{0,24},{4,28},{8,16},{12,20},{16,8},{20,12},{24,0},{28,4},{1,25},{... | collective-permute-start | bytes 393224 | tf_op jit(solution)/shard_map/ppermute | solution.py:235
  218.2 44.8 %collective-permute-start.28 = (bf16[512,2176]{1,0:T(8,128)(2,1)S(1)}, bf16[512,2176]{1,0:T(8,128)(2,1)}, u32[]{:S(2)}, u32[]{:S(2)}) collective-permute-start(bf16[512,2176]{1,0:T(8,128)(2,1)S(1)} %collective-permute-done.22.refs_2_), channel_id=1, source_target_pairs={{0,4},{4,0},{8,12},{12,8},{16,20},{20,16},{24,28},{28,24},{1,5},{5... | collective-permute-start | bytes 6684680 | tf_op jit(solution)/shard_map/ppermute | solution.py:235
  219.8 43.2 %collective-permute-start.24 = (f32[16,2048]{1,0:T(8,128)S(1)}, f32[16,2048]{1,0:T(8,128)S(1)}, u32[]{:S(2)}, u32[]{:S(2)}) collective-permute-start(f32[16,2048]{1,0:T(8,128)S(1)} %add_add_fusion), channel_id=1, source_target_pairs={{0,1},{1,0},{2,3},{3,2},{4,5},{5,4},{6,7},{7,6},{8,9},{9,8},{10,11... | collective-permute-start | bytes 393224 | tf_op jit(solution)/shard_map/ppermute | solution.py:290
  221.2 41.8 %collective-permute-start.25 = (f32[16,2048]{1,0:T(8,128)S(1)}, f32[16,2048]{1,0:T(8,128)S(1)}, u32[]{:S(2)}, u32[]{:S(2)}) collective-permute-start(f32[16,2048]{1,0:T(8,128)S(1)} %add_add_fusion), channel_id=1, source_target_pairs={{0,2},{1,3},{2,0},{3,1},{4,6},{5,7},{6,4},{7,5},{8,10},{9,11},{10,... | collective-permute-start | bytes 393224 | tf_op jit(solution)/shard_map/ppermute | solution.py:290
  223.8 39.2 %collective-permute-start.26 = (f32[16,2048]{1,0:T(8,128)S(1)}, f32[16,2048]{1,0:T(8,128)S(1)}, u32[]{:S(2)}, u32[]{:S(2)}) collective-permute-start(f32[16,2048]{1,0:T(8,128)S(1)} %add_add_fusion), channel_id=1, source_target_pairs={{0,3},{1,2},{2,1},{3,0},{4,7},{5,6},{6,5},{7,4},{8,11},{9,10},{10,... | collective-permute-start | bytes 393224 | tf_op jit(solution)/shard_map/ppermute | solution.py:290
  224.4 38.7 %collective-permute-start.27 = (bf16[256,2176]{1,0:T(8,128)(2,1)S(1)}, bf16[256,2176]{1,0:T(8,128)(2,1)S(1)}, u32[]{:S(2)}, u32[]{:S(2)}) collective-permute-start(bf16[256,2176]{1,0:T(8,128)(2,1)S(1)} %slice.31), channel_id=1, source_target_pairs={{0,16},{4,12},{8,24},{12,4},{16,0},{20,28},{24,8},{28,20},{1,17},{... | collective-permute-start | bytes 3342344 | tf_op jit(solution)/shard_map/ppermute | solution.py:235
  (21 other events, 247.0 us)
Sparse Core Ops, SparseCore 0:
  151.9 66.8 reduce-scatter.2
  223.1 51.3 reduce-scatter.4
